TPU v7x, 32 devices: a whole 2x2x4 slice. The times are simulated.
32 devices in a mesh: tm: 4 (over y, core), chan: 8 (over z, x).
Axes of the slice: x: 2, y: 2, z: 4, core: 2. Of those that a mesh axis runs over, the one named last changes fastest.
Arguments:
- recordings: float32 [4, 256, 8, 512], P('tm', None, 'chan')
- gap_start: int32 [4, 256, 8], P('tm', None, 'chan'), may hold values from 0 to 511
- dropout_extent: int32 [4, 256, 8], P('tm', None, 'chan'), may hold values from 0 to 256
- filter_taps: float32 [128], replicated, may hold values from -0.5 to 0.5
- source_channel: int32 [32], P('chan'), may hold values from 0 to 255
- receiver_block: int32 [32], P('chan'), may hold values from 0 to 3
Outputs:
- stacks: float32 [128, 32, 1024], P('tm', 'chan')
All inputs are finite; a program needn't handle non-finite values.
Results may differ from a plain program's by a relative error of at most 0.0031.
Values may be sent and summed in bfloat16 or wider, within the bound.
No kernel may reach another device: no remote copies, remote signals or barrier semaphores. Data moves between devices by JAX's collectives and lax.ppermute only.
A program may use at most 64 MiB of HBM per device.

v0:
```python
import math
import jax
import jax.numpy as jnp
import numpy as np
from jax import lax
from jax.sharding import PartitionSpec as P

BLOCK = 128
MAX_LAG = 512


def passed_along(block, axis, distance):
    devices = range(lax.axis_size(axis))
    route = [(i - distance, i) for i in devices if i - distance in devices]
    return lax.ppermute(block, axis, route)


def valid_mask(starts, lengths, sample_count):
    position = jnp.arange(sample_count, dtype=jnp.int32)
    inside = (position >= starts[..., None]) & (position < starts[..., None] + lengths[..., None])
    return jnp.where(inside, 0.0, 1.0).astype(jnp.float32)


def fir_filter(signal, filter_taps):
    tap_count = filter_taps.shape[0]
    channel_count, sample_count = signal.shape
    pieces = signal.reshape(channel_count, sample_count // tap_count, tap_count)
    earlier = jnp.concatenate([jnp.zeros_like(pieces[:, :1]), pieces[:, :-1]], axis=1)
    position = jnp.arange(tap_count, dtype=jnp.int32)
    offset = position[None, :] - position[:, None]
    present_filter_tap = jnp.where(
        offset >= 0, filter_taps[jnp.clip(offset, 0, tap_count - 1)], 0.0
    )
    carried_tap = jnp.where(
        offset < 0, filter_taps[jnp.clip(offset + tap_count, 0, tap_count - 1)], 0.0
    )
    result = jnp.einsum("cki,im->ckm", pieces, present_filter_tap, precision=lax.Precision.HIGHEST)
    result = result + jnp.einsum(
        "cki,im->ckm", earlier, carried_tap, precision=lax.Precision.HIGHEST
    )
    return result.reshape(channel_count, sample_count)


def normalize_traces(filtered, retained_mask):
    counted = jnp.sum(retained_mask, axis=-1, keepdims=True)
    mean_square = jnp.sum(filtered * filtered * retained_mask, axis=-1, keepdims=True) / counted
    return (filtered * retained_mask * lax.rsqrt(mean_square + 1e-05)).astype(jnp.bfloat16)


def correlate_batch(sources, receivers, max_lag):
    sample_count = sources.shape[-1]
    tile_width = math.gcd(math.gcd(max_lag, sample_count), 128)
    tile_count = sample_count // tile_width + 1
    edge = jnp.zeros((sources.shape[0], tile_width), sources.dtype)
    source_padded = jnp.concatenate([edge, sources, edge], axis=1)
    row_table = (
        np.arange(tile_count * tile_width)[:, None] - np.arange(tile_width)[None, :] + tile_width
    )
    lag_tiles = source_padded[:, row_table]
    lag_pad = jnp.zeros((receivers.shape[0], receivers.shape[1], max_lag), receivers.dtype)
    receivers_padded = jnp.concatenate([lag_pad, receivers, lag_pad], axis=2)
    columns = []
    for lag_block in range(2 * max_lag // tile_width):
        segment_taper = receivers_padded[
            :, :, lag_block * tile_width : lag_block * tile_width + tile_count * tile_width
        ]
        columns.append(
            jnp.einsum("scz,szu->csu", segment_taper, lag_tiles, preferred_element_type=jnp.float32)
        )
    return jnp.concatenate(columns, axis=2)


def select_blocks(blocks, receiver_block, pair_count):
    picked = [
        lax.dynamic_slice_in_dim(blocks, receiver_block[pair_index], 1, axis=0)
        for pair_index in range(pair_count)
    ]
    return jnp.concatenate(picked, axis=0)


def neighbour_blocks(owned_rows):
    return passed_along(owned_rows, "chan", -1)


def local(recordings, gap_start, dropout_extent, filter_taps, source_channel, receiver_block):
    traces = recordings[0, :, 0, :]
    retained_mask = valid_mask(gap_start[0, :, 0], dropout_extent[0, :, 0], traces.shape[1])
    filtered = fir_filter(traces * retained_mask, filter_taps)
    normalized = normalize_traces(filtered, retained_mask)
    round_count, sample_count = normalized.shape
    regrouped = lax.all_to_all(
        normalized.reshape(round_count, 1, sample_count),
        "chan",
        split_axis=0,
        concat_axis=1,
        tiled=True,
    )
    owned_rows = regrouped.reshape(round_count, sample_count)
    sources = owned_rows[source_channel]
    segment_count = lax.axis_size("tm")
    factor = 1.0 / math.sqrt(sample_count * segment_count)
    pair_count = sources.shape[0]
    block_count = round_count // BLOCK
    following = neighbour_blocks(owned_rows)
    blocks = jnp.concatenate([owned_rows, following], axis=0).reshape(
        2 * block_count, BLOCK, sample_count
    )
    receivers = select_blocks(blocks, receiver_block, pair_count)
    stack_terms = correlate_batch(sources, receivers, MAX_LAG) * factor
    stacks = lax.psum_scatter(stack_terms, "tm", scatter_dimension=0, tiled=True)
    return stacks


def solution(mesh):
    return jax.shard_map(
        local,
        mesh=mesh,
        in_specs=(
            P("tm", None, "chan", None),
            P("tm", None, "chan"),
            P("tm", None, "chan"),
            P(),
            P("chan"),
            P("chan"),
        ),
        out_specs=P("tm", "chan", None),
        check_vma=False,
    )
```

profile of v0, /device:TPU:0, one launch (start us, length us, event | category | flops | bytes accessed | tf_op | source)
XLA Modules:
  0.0 605.1 jit_solution(15314912430270999718)
XLA Ops:
  6.5 0.0 copy-start
  6.6 1.2 copy.46
  7.9 0.0 copy-done
  7.9 97.2 %gather_fusion = f32[16384]{0:T(1024)S(1)} fusion(f32[128]{0:T(128)S(1)} %copy-done, s32[16384]{0:T(1024)S(1)} %fusion.21), kind=kCustom, calls=%fused_computation | custom fusion | bytes 196608 | tf_op jit(solution)/shard_map/gather | solution.py:32
  105.1 0.0 copy-start.2
  105.1 0.0 copy-start.4
  105.1 97.2 %gather_fusion.1 = f32[16384]{0:T(1024)S(1)} fusion(f32[128]{0:T(128)S(1)} %copy-done, s32[16384]{0:T(1024)S(1)} %fusion.23), kind=kCustom, calls=%fused_computation.1 | custom fusion | bytes 196608 | tf_op jit(solution)/shard_map/gather | solution.py:35
  202.3 0.0 copy-done.2
  202.3 0.0 copy-done.4
  202.4 0.2 select_reduce_fusion
  202.6 0.2 select_multiply_fusion.1
  202.8 0.6 fusion.25
  203.4 0.0 copy-start.1
  203.4 0.7 fusion.16
  204.2 0.0 copy-start.5
  204.2 0.2 copy.63
  204.4 0.2 multiply_convert_fusion
  204.6 0.5 broadcast.235
  205.1 0.0 copy-start.3
  205.1 0.8 reduce.1
  205.9 0.9 reshape.270
  206.8 7.2 %all-to-all-start = ((bf16[8,2,8192]{2,1,0:T(2,128)(2,1)}), bf16[8,2,8192]{2,1,0:T(2,128)(2,1)S(1)}, u32[]{:S(2)}, u32[]{:S(2)}) async-start(bf16[8,2,8192]{2,1,0:T(2,128)(2,1)} %reshape.270), calls=%async_computation | async-start | bytes 524288 | tf_op jit(solution)/shard_map/all_to_all | solution.py:91
  214.0 0.0 all-reduce.6.cloned.1.call-start
  214.1 0.0 copy-done.1
  214.2 0.0 copy-done.5
  214.2 8.8 %all-to-all-done = bf16[8,2,8192]{2,1,0:T(2,128)(2,1)S(1)} async-done(((bf16[8,2,8192]{2,1,0:T(2,128)(2,1)}), bf16[8,2,8192]{2,1,0:T(2,128)(2,1)S(1)}, u32[]{:S(2)}, u32[]{:S(2)}) %all-to-all-start) | async-done | bytes 262176 | tf_op jit(solution)/shard_map/all_to_all | solution.py:91
  223.0 0.3 reshape.271
  223.3 0.2 copy.66
  223.4 1.3 collective-permute-start
  224.7 0.0 copy-done.3
  224.8 0.7 fusion.47
  233.0 0.6 gather_fusion.2
  233.6 0.2 copy.54
  233.8 286.2 %gather_fusion.3 = bf16[81920,4]{1,0:T(8,128)(2,1)} fusion(bf16[4,768]{0,1:T(8,128)(2,1)S(1)} %copy.54, s32[81920]{0:T(1024)S(1)} %broadcast_clamp_fusion), kind=kCustom, calls=%fused_computation.3 | custom fusion | bytes 1638400 | tf_op jit(solution)/shard_map/gather | solution.py:59
  520.0 19.5 %copy.55 = bf16[640,128,4]{0,1,2:T(8,128)(2,1)S(1)} copy(bf16[640,128,4]{2,1,0:T(8,128)(2,1)} %bitcast.95) | data formatting | bytes 1310720 | tf_op jit(solution)/shard_map/gather | solution.py:59
  539.5 0.0 collective-permute-done
  539.6 0.1 pad_maximum_fusion.1
  539.6 0.3 fusion.7
  540.0 0.3 fusion.6
  540.3 0.3 fusion.5
  540.6 0.4 fusion.4
  541.0 0.4 fusion.3
  541.4 0.3 fusion.2
  541.7 0.3 fusion.1
  542.1 0.3 fusion
  542.4 0.2 broadcast_multiply_fusion
  542.6 2.0 copy.56
  544.6 0.0 copy-start.6
  544.6 0.0 all-reduce.6.cloned.1.call-update
  544.7 0.6 copy-done.6
  545.3 0.6 dynamic-slice
  546.5 49.9 %all-reduce.6.cloned.1.call-done = f32[128,4,1024]{2,1,0:T(4,128)} async-done(((f32[128,4,1024]{2,1,0:T(4,128)}), f32[128,4,1024]{2,1,0:T(4,128)}) %all-reduce.6.cloned.1.call-update) | async-done | bytes 2097168
  596.4 1.9 constant_dynamic-slice_fusion.4
  (13 shorter events, 0.3 us)
Async XLA Ops:
  6.5 1.3 copy-start
  105.1 97.2 %copy-start.2 = (s32[1,256,1]{1,2,0:T(1,128)S(1)}, s32[1,256,1]{1,2,0:T(1,128)}, u32[]{:S(2)}) copy-start(s32[1,256,1]{1,2,0:T(1,128)} %param.9) | copy-start | bytes 3076
  105.1 97.2 %copy-start.4 = (s32[1,256,1]{1,2,0:T(1,128)S(1)}, s32[1,256,1]{1,2,0:T(1,128)}, u32[]{:S(2)}) copy-start(s32[1,256,1]{1,2,0:T(1,128)} %param.10) | copy-start | bytes 3076
  203.4 10.7 %copy-start.1 = (s32[81920]{0:T(1024)S(1)}, s32[81920]{0:T(1024)}, u32[]{:S(2)}) copy-start(s32[81920]{0:T(1024)} %constant.48) | copy-start | bytes 983044
  204.2 10.0 %copy-start.5 = (s32[4]{0:T(128)S(1)}, s32[4]{0:T(128)}, u32[]{:S(2)}) copy-start(s32[4]{0:T(128)} %param.12) | copy-start | bytes 52
  205.1 19.6 %copy-start.3 = (s32[4]{0:T(128)S(1)}, s32[4]{0:T(128)}, u32[]{:S(2)}) copy-start(s32[4]{0:T(128)} %param.13) | copy-start | bytes 52
  206.8 16.2 %all-to-all-start = ((bf16[8,2,8192]{2,1,0:T(2,128)(2,1)}), bf16[8,2,8192]{2,1,0:T(2,128)(2,1)S(1)}, u32[]{:S(2)}, u32[]{:S(2)}) async-start(bf16[8,2,8192]{2,1,0:T(2,128)(2,1)} %reshape.270), calls=%async_computation | async-start | bytes 524288 | tf_op jit(solution)/shard_map/all_to_all | solution.py:91
  214.0 382.4 %all-reduce.6.cloned.1.call-start = ((), (), s32[]{:S(2)}) async-start(), calls=%async_computation.1 | async-start | bytes 4194304
  223.4 316.0 %collective-permute-start = (bf16[256,512]{1,0:T(8,128)(2,1)S(1)}, bf16[256,512]{1,0:T(8,128)(2,1)S(1)}, u32[]{:S(2)}, u32[]{:S(2)}) collective-permute-start(bf16[256,512]{1,0:T(8,128)(2,1)S(1)} %bitcast.99), channel_id=1, source_target_pairs={{1,0},{2,1},{3,2},{4,3},{5,4},{6,5},{7,6},{9,8},{10,9},{11,10},{12... | collective-permute-start | bytes 786440 | tf_op jit(solution)/shard_map/ppermute | solution.py:15
  544.6 0.7 copy-start.6
Sparse Core Ops, SparseCore 0:
  544.8 51.5 all-reduce.5
where the time goes:
time: 606 us; the launch traced here: 605 us
  local copies, waits for them, and re-layouts  510 us (84%)
  waiting for transfers between devices  58.7 us (10%)
  between operations  21.9 us (4%)
  starting transfers between devices  8.58 us (1%)
    gather x2, local copies, waits for them, and re-layouts, correlate_batch(): lag_tiles = source_padded[:, row_table]  306 us
    gather x1, local copies, waits for them, and re-layouts, fir_filter(): filter_taps[jnp.clip(offset, 0, tap_count - 1)]  97.2 us
    gather x1, local copies, waits for them, and re-layouts, fir_filter(): filter_taps[jnp.clip(offset + tap_count, 0, tap_count - 1)]  97.2 us
    unnamed x2, waiting for transfers between devices  49.9 us
  transfers between devices with their start and end apart: 3, of which 2 were waited for; matrix products, arithmetic and copies ran while one was open for 51% of the time, Pallas kernels for 0%

commit v1 on v0

--- a/solution.py
+++ b/solution.py
@@ -88,13 +88,20 @@
     filtered = fir_filter(traces * retained_mask, filter_taps)
     normalized = normalize_traces(filtered, retained_mask)
     round_count, sample_count = normalized.shape
-    regrouped = lax.all_to_all(
-        normalized.reshape(round_count, 1, sample_count),
-        "chan",
-        split_axis=0,
-        concat_axis=1,
-        tiled=True,
-    )
+    x = normalized.reshape(round_count, 1, sample_count)
+    ways, here = (lax.axis_size("chan"), lax.axis_index("chan"))
+    width = x.shape[0] // ways
+    lengths_2 = list(x.shape)
+    lengths_2[0] = width
+    height = lengths_2[1]
+    lengths_2[1] = height * ways
+    full = jnp.zeros(lengths_2, x.dtype)
+    for mask in range(ways):
+        part = lax.dynamic_slice_in_dim(x, (here ^ mask) * width, width, axis=0)
+        if mask:
+            part = lax.ppermute(part, "chan", [(d, d ^ mask) for d in range(ways)])
+        full = lax.dynamic_update_slice_in_dim(full, part, (here ^ mask) * height, axis=1)
+    regrouped = full
     owned_rows = regrouped.reshape(round_count, sample_count)
     sources = owned_rows[source_channel]
     segment_count = lax.axis_size("tm")

time: 606 us -> 605 us (level)
  waiting for transfers between devices: 58.7 us -> 52.3 us
    ppermute x0 -> x7, starting transfers between devices: none -> 12.6 us  [local(): part = lax.ppermute(part, 'chan', [(d, d ^ mask) for d in range(ways)])]
    all_to_all x1 -> x0, waiting for transfers between devices: 8.79 us -> none  [local(): lax.all_to_all(normalized.reshape(round_count, 1, sample_count), 'chan',...]
    all_to_all x1 -> x0, starting transfers between devices: 7.25 us -> none  [local(): lax.all_to_all(normalized.reshape(round_count, 1, sample_count), 'chan',...]
  transfers between devices with their start and end apart: 3 -> 9, of which waited for: 2 -> 2; matrix products, arithmetic and copies ran while one was open for 51% -> 51% of each run, Pallas kernels for 0% -> 0%
where the time goes in v1:
time: 605 us
  local copies, waits for them, and re-layouts  511 us (84%)
  waiting for transfers between devices  52.3 us (9%)
  between operations  22 us (4%)
  starting transfers between devices  13.9 us (2%)
    gather x2, local copies, waits for them, and re-layouts, correlate_batch(): lag_tiles = source_padded[:, row_table]  304 us
    gather x1, local copies, waits for them, and re-layouts, fir_filter(): filter_taps[jnp.clip(offset + tap_count, 0, tap_count - 1)]  97.2 us
    gather x1, local copies, waits for them, and re-layouts, fir_filter(): filter_taps[jnp.clip(offset, 0, tap_count - 1)]  97.2 us
    unnamed x2, waiting for transfers between devices  50.5 us
    ppermute x7, starting transfers between devices, local(): part = lax.ppermute(part, 'chan', [(d, d ^ mask) for d in range(ways)])  12.6 us
  transfers between devices with their start and end apart: 9, of which 2 were waited for; matrix products, arithmetic and copies ran while one was open for 51% of the time, Pallas kernels for 0%

profile of v1, /device:TPU:0, one launch (start us, length us, event | category | flops | bytes accessed | tf_op | source)
XLA Modules:
  0.0 604.6 jit_solution(15951015988526309096)
XLA Ops:
  6.7 1.2 copy.32
  7.9 97.2 %gather_fusion = f32[16384]{0:T(1024)S(1)} fusion(f32[128]{0:T(128)S(1)} %copy-done, s32[16384]{0:T(1024)S(1)} %fusion.22), kind=kCustom, calls=%fused_computation | custom fusion | bytes 196608 | tf_op jit(solution)/shard_map/gather | solution.py:32
  105.1 0.0 copy-start.2
  105.2 0.0 copy-start.4
  105.2 97.2 %gather_fusion.1 = f32[16384]{0:T(1024)S(1)} fusion(f32[128]{0:T(128)S(1)} %copy-done, s32[16384]{0:T(1024)S(1)} %fusion.24), kind=kCustom, calls=%fused_computation.1 | custom fusion | bytes 196608 | tf_op jit(solution)/shard_map/gather | solution.py:35
  202.4 0.2 select_reduce_fusion
  202.6 0.2 select_multiply_fusion.2
  202.8 0.6 fusion.26
  203.4 0.0 copy-start.1
  203.5 0.0 copy-start.5
  203.5 0.7 fusion.16
  204.2 0.2 copy.37
  204.4 0.0 copy-start.3
  204.4 0.2 fusion.18
  204.7 3.0 collective-permute-start
  207.7 1.6 collective-permute-start.1
  209.3 0.0 collective-permute-start.2
  209.3 3.0 collective-permute-start.3
  212.3 1.3 collective-permute-start.4
  213.7 3.7 collective-permute-start.5
  217.3 0.0 collective-permute-done.1
  217.3 0.1 collective-permute-start.6
  217.4 0.1 copy.38
  217.5 0.6 dynamic_update_slice.24
  218.1 0.1 copy.39
  218.2 0.6 dynamic_update_slice.25
  218.8 0.1 copy.40
  218.9 0.6 dynamic_update_slice.26
  219.5 0.0 collective-permute-done.2
  219.5 0.1 copy.41
  219.5 0.6 dynamic_update_slice.27
  220.2 0.1 copy.42
  220.2 0.6 dynamic_update_slice.28
  220.8 0.0 collective-permute-done.4
  220.8 0.1 copy.43
  220.9 0.6 dynamic_update_slice.29
  221.5 0.1 copy.44
  221.6 0.6 dynamic_update_slice.30
  222.2 1.7 collective-permute-done.6
  223.9 0.1 copy.45
  224.0 0.6 dynamic_update_slice.31
  224.6 1.3 collective-permute-start.7
  225.9 0.6 fusion.48
  234.0 0.6 gather_fusion.2
  234.5 0.2 copy.46
  234.7 284.2 %gather_fusion.3 = bf16[81920,4]{1,0:T(8,128)(2,1)} fusion(bf16[4,768]{0,1:T(8,128)(2,1)S(1)} %copy.46, s32[81920]{0:T(1024)S(1)} %broadcast_clamp_fusion), kind=kCustom, calls=%fused_computation.3 | custom fusion | bytes 1638400 | tf_op jit(solution)/shard_map/gather | solution.py:59
  518.9 19.5 %copy.47 = bf16[640,128,4]{0,1,2:T(8,128)(2,1)S(1)} copy(bf16[640,128,4]{2,1,0:T(8,128)(2,1)} %bitcast.106) | data formatting | bytes 1310720 | tf_op jit(solution)/shard_map/gather | solution.py:59
  538.4 0.0 collective-permute-done.7
  538.5 0.1 pad_maximum_fusion.1
  538.6 0.3 fusion.7
  538.9 0.3 fusion.6
  539.2 0.3 fusion.5
  539.5 0.4 fusion.4
  539.9 0.4 fusion.3
  540.3 0.3 fusion.2
  540.7 0.3 fusion.1
  541.0 0.3 fusion
  541.3 0.2 broadcast_multiply_fusion
  541.5 2.0 copy.48
  543.6 0.0 all-reduce.6.cloned.1.call-update
  543.6 0.6 copy-done.6
  544.2 0.6 dynamic-slice.32
  545.4 50.5 %all-reduce.6.cloned.1.call-done = f32[128,4,1024]{2,1,0:T(4,128)} async-done(((f32[128,4,1024]{2,1,0:T(4,128)}), f32[128,4,1024]{2,1,0:T(4,128)}) %all-reduce.6.cloned.1.call-update) | async-done | bytes 2097168
  595.9 1.9 constant_dynamic-slice_fusion.4
  (26 shorter events, 0.3 us)
Async XLA Ops:
  6.5 1.4 copy-start
  6.5 589.4 %all-reduce.6.cloned.1.call-start = ((), (), s32[]{:S(2)}) async-start(), calls=%async_computation | async-start | bytes 4194304
  105.1 97.2 %copy-start.2 = (s32[1,256,1]{1,2,0:T(1,128)S(1)}, s32[1,256,1]{1,2,0:T(1,128)}, u32[]{:S(2)}) copy-start(s32[1,256,1]{1,2,0:T(1,128)} %param.9) | copy-start | bytes 3076
  105.2 97.2 %copy-start.4 = (s32[1,256,1]{1,2,0:T(1,128)S(1)}, s32[1,256,1]{1,2,0:T(1,128)}, u32[]{:S(2)}) copy-start(s32[1,256,1]{1,2,0:T(1,128)} %param.10) | copy-start | bytes 3076
  203.4 10.2 %copy-start.1 = (s32[81920]{0:T(1024)S(1)}, s32[81920]{0:T(1024)}, u32[]{:S(2)}) copy-start(s32[81920]{0:T(1024)} %constant.70) | copy-start | bytes 983044
  203.5 13.9 %copy-start.5 = (s32[4]{0:T(128)S(1)}, s32[4]{0:T(128)}, u32[]{:S(2)}) copy-start(s32[4]{0:T(128)} %param.12) | copy-start | bytes 52
  204.4 21.5 %copy-start.3 = (s32[4]{0:T(128)S(1)}, s32[4]{0:T(128)}, u32[]{:S(2)}) copy-start(s32[4]{0:T(128)} %param.13) | copy-start | bytes 52
  204.7 8.9 %collective-permute-start = (bf16[32,1,512]{2,0,1:T(8,128)(2,1)S(1)}, bf16[32,1,512]{2,0,1:T(8,128)(2,1)S(1)}, u32[]{:S(2)}, u32[]{:S(2)}) collective-permute-start(bf16[32,1,512]{2,0,1:T(8,128)(2,1)S(1)} %get-tuple-element.15), channel_id=1, source_target_pairs={{0,1},{1,0},{2,3},{3,2},{4,5},{5,4},{6,7},{7,6},{8,9},{9,8},{10,11... | collective-permute-start | bytes 98312 | tf_op jit(solution)/shard_map/ppermute | solution.py:102
  207.7 9.6 %collective-permute-start.1 = (bf16[32,1,512]{2,0,1:T(8,128)(2,1)S(1)}, bf16[32,1,512]{2,0,1:T(8,128)(2,1)S(1)}, u32[]{:S(2)}, u32[]{:S(2)}) collective-permute-start(bf16[32,1,512]{2,0,1:T(8,128)(2,1)S(1)} %get-tuple-element.14), channel_id=1, source_target_pairs={{0,2},{1,3},{2,0},{3,1},{4,6},{5,7},{6,4},{7,5},{8,10},{9,11},{10,... | collective-permute-start | bytes 98312 | tf_op jit(solution)/shard_map/ppermute | solution.py:102
  209.3 10.2 %collective-permute-start.2 = (bf16[32,1,512]{2,0,1:T(8,128)(2,1)S(1)}, bf16[32,1,512]{2,0,1:T(8,128)(2,1)S(1)}, u32[]{:S(2)}, u32[]{:S(2)}) collective-permute-start(bf16[32,1,512]{2,0,1:T(8,128)(2,1)S(1)} %get-tuple-element.13), channel_id=1, source_target_pairs={{0,3},{1,2},{2,1},{3,0},{4,7},{5,6},{6,5},{7,4},{8,11},{9,10},{10,... | collective-permute-start | bytes 98312 | tf_op jit(solution)/shard_map/ppermute | solution.py:102
  209.3 10.8 %collective-permute-start.3 = (bf16[32,1,512]{2,0,1:T(8,128)(2,1)S(1)}, bf16[32,1,512]{2,0,1:T(8,128)(2,1)S(1)}, u32[]{:S(2)}, u32[]{:S(2)}) collective-permute-start(bf16[32,1,512]{2,0,1:T(8,128)(2,1)S(1)} %get-tuple-element.12), channel_id=1, source_target_pairs={{0,4},{1,5},{2,6},{3,7},{4,0},{5,1},{6,2},{7,3},{8,12},{9,13},{10,... | collective-permute-start | bytes 98312 | tf_op jit(solution)/shard_map/ppermute | solution.py:102
  212.3 8.5 %collective-permute-start.4 = (bf16[32,1,512]{2,0,1:T(8,128)(2,1)S(1)}, bf16[32,1,512]{2,0,1:T(8,128)(2,1)S(1)}, u32[]{:S(2)}, u32[]{:S(2)}) collective-permute-start(bf16[32,1,512]{2,0,1:T(8,128)(2,1)S(1)} %get-tuple-element.11), channel_id=1, source_target_pairs={{0,5},{1,4},{2,7},{3,6},{4,1},{5,0},{6,3},{7,2},{8,13},{9,12},{10,... | collective-permute-start | bytes 98312 | tf_op jit(solution)/shard_map/ppermute | solution.py:102
  213.7 7.9 %collective-permute-start.5 = (bf16[32,1,512]{2,0,1:T(8,128)(2,1)S(1)}, bf16[32,1,512]{2,0,1:T(8,128)(2,1)S(1)}, u32[]{:S(2)}, u32[]{:S(2)}) collective-permute-start(bf16[32,1,512]{2,0,1:T(8,128)(2,1)S(1)} %get-tuple-element.10), channel_id=1, source_target_pairs={{0,6},{1,7},{2,4},{3,5},{4,2},{5,3},{6,0},{7,1},{8,14},{9,15},{10,... | collective-permute-start | bytes 98312 | tf_op jit(solution)/shard_map/ppermute | solution.py:102
  217.3 6.6 %collective-permute-start.6 = (bf16[32,1,512]{2,0,1:T(8,128)(2,1)S(1)}, bf16[32,1,512]{2,0,1:T(8,128)(2,1)S(1)}, u32[]{:S(2)}, u32[]{:S(2)}) collective-permute-start(bf16[32,1,512]{2,0,1:T(8,128)(2,1)S(1)} %get-tuple-element.9), channel_id=1, source_target_pairs={{0,7},{1,6},{2,5},{3,4},{4,3},{5,2},{6,1},{7,0},{8,15},{9,14},{10,... | collective-permute-start | bytes 98312 | tf_op jit(solution)/shard_map/ppermute | solution.py:102
  224.6 313.8 %collective-permute-start.7 = (bf16[256,512]{1,0:T(8,128)(2,1)S(1)}, bf16[256,512]{1,0:T(8,128)(2,1)S(1)}, u32[]{:S(2)}, u32[]{:S(2)}) collective-permute-start(bf16[256,512]{1,0:T(8,128)(2,1)S(1)} %bitcast.110), channel_id=1, source_target_pairs={{1,0},{2,1},{3,2},{4,3},{5,4},{6,5},{7,6},{9,8},{10,9},{11,10},{12... | collective-permute-start | bytes 786440 | tf_op jit(solution)/shard_map/ppermute | solution.py:15
  543.6 0.7 copy-start.6
Sparse Core Ops, SparseCore 0:
  543.7 52.1 all-reduce.5
